TPU v7x, 128 devices: a whole 4x4x4 slice. The times are simulated.
128 devices in a mesh: ctx: 32 (over y_hi, x, z), fsdp: 4 (over y_lo, core).
Axes of the slice: x: 4, y: 4 (y_hi: 2, y_lo: 2; y = y_hi * 2 + y_lo), z: 4, core: 2. Of those that a mesh axis runs over, the one named last changes fastest.
Arguments:
- layer_input: bfloat16 [4, 4096, 1024], P('fsdp', 'ctx'), may hold values from -6 to 6
- cotangent: bfloat16 [4, 4096, 1024], P('fsdp', 'ctx'), may hold values from -6 to 6
- block_order: int32 [4, 64], P('fsdp'), may hold values from 0 to 63, as said below
- query_weight: bfloat16 [1024, 2048], P('fsdp'), may hold values from -0.1875 to 0.1875
- key_projection: bfloat16 [1024, 1024], P('fsdp'), may hold values from -0.1875 to 0.1875
- value_projection: bfloat16 [1024, 1024], P('fsdp'), may hold values from -0.1875 to 0.1875
- output_weight: bfloat16 [2048, 1024], P('fsdp'), may hold values from -0.75 to 0.75
- gate_weight: bfloat16 [1024, 3072], P('fsdp'), may hold values from -0.1875 to 0.1875
- up_weight: bfloat16 [1024, 3072], P('fsdp'), may hold values from -0.1875 to 0.1875
- down_weight: bfloat16 [3072, 1024], P('fsdp'), may hold values from -0.109375 to 0.109375
- first_gain: float32 [1024], replicated, may hold values from 0.5 to 1.5
- second_gain: float32 [1024], replicated, may hold values from 0.5 to 1.5
- query_gain: float32 [128], replicated, may hold values from 0.25 to 1.75
- key_norm_gain: float32 [128], replicated, may hold values from 0.25 to 1.75
Outputs:
- layer_output: bfloat16 [4, 4096, 1024], P('fsdp', 'ctx')
- input_gradient: float32 [4, 4096, 1024], P('fsdp', 'ctx')
- query_weight_gradient: float32 [1024, 2048], P('fsdp')
- key_weight_gradient: float32 [1024, 1024], P('fsdp')
- value_weight_gradient: float32 [1024, 1024], P('fsdp')
- output_weight_gradient: float32 [2048, 1024], P('fsdp')
- gate_weight_gradient: float32 [1024, 3072], P('fsdp')
- up_weight_gradient: float32 [1024, 3072], P('fsdp')
- down_weight_gradient: float32 [3072, 1024], P('fsdp')
- first_gain_gradient: float32 [1024], P('fsdp')
- second_gain_gradient: float32 [1024], P('fsdp')
- query_gain_gradient: float32 [128], P('fsdp')
- key_gain_gradient: float32 [128], P('fsdp')
Inputs may be any that keep to these rules, and one draw needn't show every extreme that they name: Each row of block_order names every block of 64 positions of its sequence exactly once; the two blocks of rows 2 c and 2 c + 1 are mirrored, block b together with block 2 * 32 - 1 - b, in either order.
All inputs are finite; a program needn't handle non-finite values.
Results may differ from a plain program's by a relative error of at most 0.034.
Values may be sent and summed in bfloat16 or wider, within the bound.
No kernel may reach another device: no remote copies, remote signals or barrier semaphores. Data moves between devices by JAX's collectives and lax.ppermute only.
A program may use at most 320 MiB of HBM per device.

v0:
```python
import math
import jax
import jax.numpy as jnp
from jax import lax
from jax.sharding import PartitionSpec as P

HQ = 16
KEY_VALUE_HEADS = 8
HEAD_SIZE = 128
CTX = ("yh", "x", "z")
FSDP = ("yl", "c")
EPSILON = 1e-06
THETA = 1000000.0
MASKED = -1e30


def rms_apply(values, norm_gain):
    row_scale = lax.rsqrt(jnp.mean(values * values, axis=-1, keepdims=True) + EPSILON)
    normed = values * row_scale
    return (normed * norm_gain, normed, row_scale)


def root_mean_square_backward(gradient, normed, row_scale, norm_gain):
    normed_grad = gradient * norm_gain
    return row_scale * (
        normed_grad - normed * jnp.mean(normed_grad * normed, axis=-1, keepdims=True)
    )


def rope_tables(positions, head_width):
    half_width = head_width // 2
    inverse_freq = jnp.power(THETA, -2.0 * jnp.arange(half_width, dtype=jnp.float32) / head_width)
    angles = positions.astype(jnp.float32)[:, None] * inverse_freq[None, :]
    return (jnp.cos(angles)[:, None, :], jnp.sin(angles)[:, None, :])


def rotary_apply(values, cosine_table, sine_values_table):
    half_width = values.shape[-1] // 2
    front_half = values[..., :half_width]
    back_half = values[..., half_width:]
    return jnp.concatenate(
        [
            front_half * cosine_table - back_half * sine_values_table,
            back_half * cosine_table + front_half * sine_values_table,
        ],
        axis=-1,
    )


def rotary_backward(gradient, cosine_table, sine_values_table):
    half_width = gradient.shape[-1] // 2
    front_half = gradient[..., :half_width]
    back_half = gradient[..., half_width:]
    return jnp.concatenate(
        [
            front_half * cosine_table + back_half * sine_values_table,
            back_half * cosine_table - front_half * sine_values_table,
        ],
        axis=-1,
    )


def left_dot(left_side, right_side):
    return lax.dot_general(
        left_side, right_side, (((0,), (0,)), ((), ())), preferred_element_type=jnp.float32
    )


def right_dot(left_side, right_side):
    return lax.dot_general(
        left_side, right_side, (((1,), (1,)), ((), ())), preferred_element_type=jnp.float32
    )


def gather_fsdp(values):
    across = lax.all_gather(values, "yl", axis=0, tiled=False)
    both = lax.all_gather(across, "c", axis=1, tiled=False)
    return both.reshape((-1,) + values.shape[1:])


def reduce_ctx(shards):
    flat = jnp.concatenate([s.astype(jnp.bfloat16).reshape(-1) for s in shards])
    lanes = 128
    step = 256 * lanes
    padded = -(-flat.shape[0] // step) * step
    flat = jnp.pad(flat, (0, padded - flat.shape[0])).reshape(padded // lanes, lanes)
    part = lax.psum_scatter(flat, "z", scatter_dimension=0, tiled=True)
    part = lax.psum_scatter(part, "x", scatter_dimension=0, tiled=True)
    part = lax.psum(part, "yh")
    part = lax.all_gather(part, "x", axis=0, tiled=True)
    full = lax.all_gather(part, "z", axis=0, tiled=True).reshape(-1)
    out = []
    at = 0
    for s in shards:
        out.append(full[at : at + s.size].reshape(s.shape).astype(jnp.float32))
        at += s.size
    return tuple(out)


def on_device(
    layer_input,
    cotangent,
    block_order,
    query_weight,
    key_projection,
    value_projection,
    output_weight,
    gate_weight,
    up_weight,
    down_weight,
    first_gain,
    second_gain,
    query_gain,
    key_norm_gain,
):
    local_rows = layer_input.shape[1]
    block_rows = local_rows // 2
    ctx_size = lax.axis_size(CTX)
    halves = ctx_size // HQ
    half_devices = ctx_size // halves
    order_row = block_order[0]
    device_place = lax.axis_index(CTX)
    my_half = device_place // half_devices
    all_positions = (
        order_row[:, None] * block_rows + jnp.arange(block_rows, dtype=jnp.int32)[None, :]
    ).reshape(-1)
    own_positions = lax.dynamic_slice_in_dim(all_positions, device_place * local_rows, local_rows)
    cosine_table, sine_values_table = rope_tables(own_positions, HEAD_SIZE)
    scale_factor = 1.0 / math.sqrt(HEAD_SIZE)
    half_rows = half_devices * local_rows
    query_positions = lax.dynamic_slice_in_dim(all_positions, my_half * half_rows, half_rows)
    allowed = all_positions[None, :] <= query_positions[:, None]
    half_select = (jnp.arange(halves, dtype=jnp.int32) == my_half)[:, None, None, None]

    def to_heads(per_head):
        by_head = jnp.transpose(per_head, (1, 0, 2))
        return jnp.where(half_select, by_head[None], jnp.zeros_like(by_head)[None]).reshape(
            ctx_size, local_rows, per_head.shape[-1]
        )

    def gather_half(received):
        return lax.dynamic_slice_in_dim(received, my_half * half_devices, half_devices, 0).reshape(
            half_rows, received.shape[-1]
        )

    def from_heads(per_head):
        blocks = per_head.reshape(half_devices, local_rows, per_head.shape[-1])
        return jnp.where(half_select, blocks[None], jnp.zeros_like(blocks)[None]).reshape(
            ctx_size, local_rows, per_head.shape[-1]
        )

    def own_heads(received):
        mine = lax.dynamic_slice_in_dim(received, my_half * half_devices, half_devices, 0)
        return jnp.transpose(mine, (1, 0, 2))

    def exchange(values):
        return lax.all_to_all(values, CTX, split_axis=0, concat_axis=0, tiled=True)

    full_query, full_key, full_value, full_output, full_gate, full_up, full_down = (
        gather_fsdp(query_weight),
        gather_fsdp(key_projection),
        gather_fsdp(value_projection),
        gather_fsdp(output_weight),
        gather_fsdp(gate_weight),
        gather_fsdp(up_weight),
        gather_fsdp(down_weight),
    )
    input_f32 = layer_input[0].astype(jnp.float32)
    gained, first_normed, first_scale = rms_apply(input_f32, first_gain)
    attention_input = gained.astype(jnp.bfloat16)
    query_pre = jnp.dot(attention_input, full_query, preferred_element_type=jnp.float32).reshape(
        local_rows, HQ, HEAD_SIZE
    )
    query_gained, query_normed, query_scale = rms_apply(query_pre, query_gain)
    query_rotated = rotary_apply(query_gained, cosine_table, sine_values_table).astype(jnp.bfloat16)
    key_before_norm = jnp.dot(
        attention_input, full_key, preferred_element_type=jnp.float32
    ).reshape(local_rows, KEY_VALUE_HEADS, HEAD_SIZE)
    key_after_gain, key_after_norm, key_norm_scale = rms_apply(key_before_norm, key_norm_gain)
    own_keys = rotary_apply(key_after_gain, cosine_table, sine_values_table).astype(jnp.bfloat16)
    own_values = (
        jnp.dot(attention_input, full_value, preferred_element_type=jnp.float32)
        .astype(jnp.bfloat16)
        .reshape(local_rows, KEY_VALUE_HEADS, HEAD_SIZE)
    )
    group = HQ // KEY_VALUE_HEADS
    key_value = jnp.repeat(jnp.concatenate([own_keys, own_values], axis=-1), group, axis=1)
    sent = jnp.concatenate(
        [to_heads(query_rotated), jnp.tile(jnp.transpose(key_value, (1, 0, 2)), (halves, 1, 1))],
        axis=-1,
    )
    received = exchange(sent)
    head_query = gather_half(received[..., :HEAD_SIZE])
    head_key = received[..., HEAD_SIZE : 2 * HEAD_SIZE].reshape(-1, HEAD_SIZE)
    head_value = received[..., 2 * HEAD_SIZE :].reshape(-1, HEAD_SIZE)

    def head_scores():
        raw_scores = (
            jnp.einsum("qd,kd->qk", head_query, head_key, preferred_element_type=jnp.float32)
            * scale_factor
        )
        return jnp.where(allowed, raw_scores, MASKED)

    raw_scores = head_scores()
    row_max = jnp.max(raw_scores, axis=-1, keepdims=True)
    log_total = row_max + jnp.log(jnp.sum(jnp.exp(raw_scores - row_max), axis=-1, keepdims=True))
    weights_b = jnp.exp(raw_scores - log_total).astype(jnp.bfloat16)
    head_mixed = jnp.dot(weights_b, head_value, preferred_element_type=jnp.float32)
    mixed_b = own_heads(exchange(from_heads(head_mixed.astype(jnp.bfloat16)))).reshape(
        local_rows, HQ * HEAD_SIZE
    )
    residual_mid = input_f32 + jnp.dot(mixed_b, full_output, preferred_element_type=jnp.float32)
    gained_mid, second_normed, second_scale = rms_apply(residual_mid, second_gain)
    mlp_in = gained_mid.astype(jnp.bfloat16)
    gate_pre = jnp.dot(mlp_in, full_gate, preferred_element_type=jnp.float32)
    up_pre = jnp.dot(mlp_in, full_up, preferred_element_type=jnp.float32)
    sigmoid_gate = jax.nn.sigmoid(gate_pre)
    silu_gate = gate_pre * sigmoid_gate
    hidden = (silu_gate * up_pre).astype(jnp.bfloat16)
    layer_output = (
        residual_mid + jnp.dot(hidden, full_down, preferred_element_type=jnp.float32)
    ).astype(jnp.bfloat16)
    own_cotangent = cotangent[0]
    hidden_grad = right_dot(own_cotangent, full_down)
    gate_grad = (
        hidden_grad * up_pre * sigmoid_gate * (1.0 + gate_pre * (1.0 - sigmoid_gate))
    ).astype(jnp.bfloat16)
    up_grad = (hidden_grad * silu_gate).astype(jnp.bfloat16)
    mlp_in_grad = right_dot(gate_grad, full_gate) + right_dot(up_grad, full_up)
    second_gain_grad = jnp.sum(mlp_in_grad * second_normed, axis=0)
    mid_grad = own_cotangent.astype(jnp.float32) + root_mean_square_backward(
        mlp_in_grad, second_normed, second_scale, second_gain
    )
    mid_grad_b = mid_grad.astype(jnp.bfloat16)
    mixed_gradient = right_dot(mid_grad_b, full_output).astype(jnp.bfloat16)
    head_out_grad = gather_half(
        exchange(to_heads(mixed_gradient.reshape(local_rows, HQ, HEAD_SIZE)))
    )
    out_grad_f = head_out_grad.astype(jnp.float32)
    delta = jnp.sum(out_grad_f * head_mixed, axis=-1, keepdims=True)
    probabilities = jnp.exp(head_scores() - log_total)
    value_part = left_dot(probabilities.astype(jnp.bfloat16), head_out_grad)
    prob_grad = right_dot(head_out_grad, head_value)
    score_grad = (probabilities * (prob_grad - delta)).astype(jnp.bfloat16)
    query_part = jnp.dot(score_grad, head_key, preferred_element_type=jnp.float32) * scale_factor
    key_part = left_dot(score_grad, head_query) * scale_factor
    returned = exchange(
        jnp.concatenate(
            [
                from_heads(query_part.astype(jnp.bfloat16)),
                jnp.concatenate([key_part, value_part], axis=-1)
                .astype(jnp.bfloat16)
                .reshape(ctx_size, local_rows, 2 * HEAD_SIZE),
            ],
            axis=-1,
        )
    )
    query_grad_rows = own_heads(returned[..., :HEAD_SIZE]).astype(jnp.float32)
    kv_parts = (
        returned[..., HEAD_SIZE:]
        .astype(jnp.float32)
        .reshape(halves, KEY_VALUE_HEADS, group, local_rows, 2 * HEAD_SIZE)
    )
    kv_grad = jnp.transpose(jnp.sum(kv_parts, axis=(0, 2)), (1, 0, 2))
    local_key_gradient = kv_grad[..., :HEAD_SIZE]
    own_value_grad = kv_grad[..., HEAD_SIZE:].reshape(local_rows, KEY_VALUE_HEADS * HEAD_SIZE)
    query_back = rotary_backward(query_grad_rows, cosine_table, sine_values_table)
    query_gain_grad = jnp.sum(query_back * query_normed, axis=(0, 1))
    query_pre_grad = (
        root_mean_square_backward(query_back, query_normed, query_scale, query_gain)
        .astype(jnp.bfloat16)
        .reshape(local_rows, HQ * HEAD_SIZE)
    )
    key_backward_pass = rotary_backward(local_key_gradient, cosine_table, sine_values_table)
    key_gain_grad = jnp.sum(key_backward_pass * key_after_norm, axis=(0, 1))
    key_before_norm_gradient = (
        root_mean_square_backward(key_backward_pass, key_after_norm, key_norm_scale, key_norm_gain)
        .astype(jnp.bfloat16)
        .reshape(local_rows, KEY_VALUE_HEADS * HEAD_SIZE)
    )
    value_gradient_second = own_value_grad.astype(jnp.bfloat16)
    attn_in_grad = (
        right_dot(query_pre_grad, full_query)
        + right_dot(key_before_norm_gradient, full_key)
        + right_dot(value_gradient_second, full_value)
    )
    first_gain_grad = jnp.sum(attn_in_grad * first_normed, axis=0)
    input_grad = mid_grad + root_mean_square_backward(
        attn_in_grad, first_normed, first_scale, first_gain
    )
    attn_cols, mixed_cols, mlp_cols, hidden_cols = (
        lax.all_to_all(attention_input, FSDP, split_axis=1, concat_axis=0, tiled=True),
        lax.all_to_all(mixed_b, FSDP, split_axis=1, concat_axis=0, tiled=True),
        lax.all_to_all(mlp_in, FSDP, split_axis=1, concat_axis=0, tiled=True),
        lax.all_to_all(hidden, FSDP, split_axis=1, concat_axis=0, tiled=True),
    )
    cot_rows, gate_rows, up_rows, mid_rows, query_rows, key_rows, value_row_block = (
        gather_fsdp(own_cotangent),
        gather_fsdp(gate_grad),
        gather_fsdp(up_grad),
        gather_fsdp(mid_grad_b),
        gather_fsdp(query_pre_grad),
        gather_fsdp(key_before_norm_gradient),
        gather_fsdp(value_gradient_second),
    )
    query_shard = left_dot(attn_cols, query_rows)
    key_shard = left_dot(attn_cols, key_rows)
    value_shard = left_dot(attn_cols, value_row_block)
    output_shard = left_dot(mixed_cols, mid_rows)
    gate_shard = left_dot(mlp_cols, gate_rows)
    up_shard = left_dot(mlp_cols, up_rows)
    down_shard = left_dot(hidden_cols, cot_rows)
    first_shard, second_shard, query_gain_shard, key_gain_shard = (
        lax.psum_scatter(first_gain_grad, FSDP, scatter_dimension=0, tiled=True),
        lax.psum_scatter(second_gain_grad, FSDP, scatter_dimension=0, tiled=True),
        lax.psum_scatter(query_gain_grad, FSDP, scatter_dimension=0, tiled=True),
        lax.psum_scatter(key_gain_grad, FSDP, scatter_dimension=0, tiled=True),
    )
    shards = (
        query_shard,
        key_shard,
        value_shard,
        output_shard,
        gate_shard,
        up_shard,
        down_shard,
        first_shard,
        second_shard,
        query_gain_shard,
        key_gain_shard,
    )
    totals = reduce_ctx(shards)
    (
        query_total,
        key_total,
        value_total,
        output_total,
        gate_total,
        up_total,
        down_total,
        first_total,
        second_total,
        query_gain_total,
        key_gain_total,
    ) = totals
    return (
        layer_output[None],
        input_grad[None],
        query_total,
        key_total,
        value_total,
        output_total,
        gate_total,
        up_total,
        down_total,
        first_total,
        second_total,
        query_gain_total,
        key_gain_total,
    )


def solution(mesh):
    in_specs = (
        P(FSDP, CTX, None),
        P(FSDP, CTX, None),
        P(FSDP, None),
        P(FSDP, None),
        P(FSDP, None),
        P(FSDP, None),
        P(FSDP, None),
        P(FSDP, None),
        P(FSDP, None),
        P(FSDP, None),
        P(),
        P(),
        P(),
        P(),
    )
    out_specs = (
        P(FSDP, CTX, None),
        P(FSDP, CTX, None),
        P(FSDP, None),
        P(FSDP, None),
        P(FSDP, None),
        P(FSDP, None),
        P(FSDP, None),
        P(FSDP, None),
        P(FSDP, None),
        P(FSDP),
        P(FSDP),
        P(FSDP),
        P(FSDP),
    )
    torus_mesh = jax.sharding.Mesh(mesh.devices.reshape(2, 4, 4, 2, 2), ("yh", "x", "z", "yl", "c"))
    return jax.shard_map(
        on_device, mesh=torus_mesh, in_specs=in_specs, out_specs=out_specs, check_vma=False
    )
```

profile of v0, /device:TPU:1, one launch (start us, length us, event | category | flops | bytes accessed | tf_op | source)
XLA Modules:
  0.0 1240.5 jit_solution(9010868726562113697)
XLA Ops:
  11.2 25.6 %all-gather.61.cloned.1.call-done = bf16[512,1024]{1,0:T(8,128)(2,1)} async-done(((bf16[256,1024]{1,0:T(8,128)(2,1)}), bf16[512,1024]{1,0:T(8,128)(2,1)}) %all-gather.61.cloned.1.call-update) | async-done | bytes 1048592 | tf_op jit(solution)/shard_map/all_gather | solution.py:76
  36.8 26.4 %all-gather.65.cloned.1.call-done = bf16[512,1024]{1,0:T(8,128)(2,1)} async-done(((bf16[256,1024]{1,0:T(8,128)(2,1)}), bf16[512,1024]{1,0:T(8,128)(2,1)}) %all-gather.65.cloned.1.call-update) | async-done | bytes 1048592 | tf_op jit(solution)/shard_map/all_gather | solution.py:76
  63.3 38.2 %all-gather.57.cloned.1.call-done = bf16[512,2048]{1,0:T(8,128)(2,1)} async-done(((bf16[256,2048]{1,0:T(8,128)(2,1)}), bf16[512,2048]{1,0:T(8,128)(2,1)}) %all-gather.57.cloned.1.call-update) | async-done | bytes 2097168 | tf_op jit(solution)/shard_map/all_gather | solution.py:76
  102.2 37.5 %all-gather.69.cloned.1.call-done = bf16[1024,1024]{1,0:T(8,128)(2,1)} async-done(((bf16[512,1024]{1,0:T(8,128)(2,1)}), bf16[1024,1024]{1,0:T(8,128)(2,1)}) %all-gather.69.cloned.1.call-update) | async-done | bytes 2097168 | tf_op jit(solution)/shard_map/all_gather | solution.py:76
  139.8 49.9 %all-gather.73.cloned.1.call-done = bf16[512,3072]{1,0:T(8,128)(2,1)} async-done(((bf16[256,3072]{1,0:T(8,128)(2,1)}), bf16[512,3072]{1,0:T(8,128)(2,1)}) %all-gather.73.cloned.1.call-update) | async-done | bytes 3145744 | tf_op jit(solution)/shard_map/all_gather | solution.py:76
  190.3 49.3 %all-gather.77.cloned.1.call-done = bf16[512,3072]{1,0:T(8,128)(2,1)} async-done(((bf16[256,3072]{1,0:T(8,128)(2,1)}), bf16[512,3072]{1,0:T(8,128)(2,1)}) %all-gather.77.cloned.1.call-update) | async-done | bytes 3145744 | tf_op jit(solution)/shard_map/all_gather | solution.py:76
  239.9 16.1 %all-gather.63.cloned.1.call-done = bf16[2,512,1024]{2,1,0:T(8,128)(2,1)} async-done(((bf16[2,256,1024]{2,1,0:T(8,128)(2,1)}), bf16[2,512,1024]{2,1,0:T(8,128)(2,1)}) %all-gather.63.cloned.1.call-update) | async-done | bytes 2097168 | tf_op jit(solution)/shard_map/all_gather | solution.py:77
  261.1 11.2 all-gather.67.cloned.1.call-done
  278.2 13.5 %all-gather.59.cloned.1.call-done = bf16[2,512,2048]{2,1,0:T(8,128)(2,1)} async-done(((bf16[2,256,2048]{2,1,0:T(8,128)(2,1)}), bf16[2,512,2048]{2,1,0:T(8,128)(2,1)}) %all-gather.59.cloned.1.call-update) | async-done | bytes 4194320 | tf_op jit(solution)/shard_map/all_gather | solution.py:77
  309.3 9.6 all-to-all-start
  319.2 56.7 %all-gather.81.cloned.1.call-done = bf16[1536,1024]{1,0:T(8,128)(2,1)} async-done(((bf16[768,1024]{1,0:T(8,128)(2,1)}), bf16[1536,1024]{1,0:T(8,128)(2,1)}) %all-gather.81.cloned.1.call-update) | async-done | bytes 3145744 | tf_op jit(solution)/shard_map/all_gather | solution.py:76
  378.2 14.4 %fusion.49 = (f32[2048]{0:T(1024)S(1)}, f32[2048,4096]{1,0:T(8,128)}) fusion(s32[2048]{0:T(1024)S(1)} %dynamic_slice.18, s32[4096]{0:T(1024)S(1)} %add.146, bf16[2048,128]{1,0:T(8,128)(2,1)S(1)} %bitcast.313, bf16[4096,128]{1,0:T(8,128)(2,1)S(1)} %bitcast.307), kind=kOutput, calls=%fused_computation.148 | convolution fusion | flops 2181036032 | bytes 35160064 | tf_op jit(solution)/shard_map/qd,kd->qk/dot_general | solution.py:199
  392.6 16.1 %exponential_reduce_fusion = f32[2048]{0:T(1024)S(1)} fusion(f32[2048]{0:T(1024)S(1)} %get-tuple-element.56, f32[2048,4096]{1,0:T(8,128)} %get-tuple-element.57, s32[2048]{0:T(1024)S(1)} %dynamic_slice.18, s32[4096]{0:T(1024)S(1)} %add.146), kind=kLoop, calls=%fused_computation.6 | loop fusion | flops 41940992 | bytes 33595392 | tf_op jit(solution)/shard_map/reduce_sum | solution.py:206
  408.7 18.5 %fusion.51 = (bf16[2048,128]{1,0:T(8,128)(2,1)S(1)}, f32[2048,128]{1,0:T(8,128)}) fusion(bf16[4096,128]{1,0:T(8,128)(2,1)S(1)} %bitcast.309, f32[2048]{0:T(1024)S(1)} %log_add_fusion, f32[2048,4096]{1,0:T(8,128)} %get-tuple-element.57, s32[2048]{0:T(1024)S(1)} %dynamic_slice.18, s32[4096]{0:T(1024)S(1)} %add.146), kind=kOutput, calls=%fused_computation.150 | convolution fusion | flops 2189688832 | bytes 36208640 | tf_op jit(solution)/shard_map/dot_general | solution.py:208
  427.6 28.8 %all_to_all.93 = bf16[32,128,128]{1,2,0:T(8,128)(2,1)S(1)} all-to-all(bf16[32,128,128]{1,2,0:T(8,128)(2,1)S(1)} %bitcast_select_fusion.3), channel_id=1, replica_groups=mesh['yh'=2,'x'=4,'z'=4,'yl'=2,'c'=2] {'yh','x','z'}, dimensions={0} | all-to-all | bytes 2097152 | tf_op jit(solution)/shard_map/all_to_all | solution.py:157
  503.5 20.3 %fusion.2 = bf16[4096,2048]{0,1:T(8,128)(2,1)} fusion(f32[2048,4096]{1,0:T(8,128)} %get-tuple-element.57, f32[2048]{0:T(1024)S(1)} %log_add_fusion, s32[4096]{0:T(1024)S(1)} %add.146, s32[2048]{0:T(1024)S(1)} %dynamic_slice.18), kind=kLoop, calls=%fused_computation.3 | loop fusion | flops 41943040 | bytes 50364416 | tf_op jit(solution)/shard_map/convert_element_type | solution.py:207
  523.8 22.6 %copy.81 = bf16[4096,2048]{1,0:T(8,128)(2,1)} copy(bf16[4096,2048]{0,1:T(8,128)(2,1)} %fusion.2) | data formatting | bytes 33554432 | tf_op jit(solution)/shard_map/dot_general | solution.py:64
  551.3 20.5 %multiply_convert_fusion = bf16[2048,4096]{1,0:T(8,128)(2,1)} fusion(f32[2048]{0:T(1024)S(1)} %multiply_reduce_fusion.2, f32[2048]{0:T(1024)S(1)} %log_add_fusion, bf16[2048,128]{1,0:T(8,128)(2,1)S(1)} %bitcast.265, bf16[4096,128]{1,0:T(8,128)(2,1)} %bitcast.310, f32[2048,4096]{1,0:T(8,128)} %get-tuple-element.57, s32[2048]{0:T(1024)S(1)} %dynamic_slice.18, ...), kind=kOutput, calls=%fused_computation.4 | convolution fusion | flops 2206203904 | bytes 51945472 | tf_op jit(solution)/shard_map/dot_general | solution.py:70
  595.0 10.3 convolution_convert_fusion.6
  618.4 44.4 %all_gather.212 = bf16[2,128,1024]{2,1,0:T(8,128)(2,1)} all-gather(bf16[1,128,1024]{2,1,0:T(8,128)(2,1)S(1)} %copy-done.15), channel_id=1, replica_groups=mesh['yh'=2,'x'=4,'z'=4,'yl'=2,'c'=2] {'yl'}, dimensions={0}, use_global_device_ids=true | all-gather | bytes 786432 | tf_op jit(solution)/shard_map/all_gather | solution.py:76
  668.0 10.4 all-gather.17
  702.2 22.3 %all_gather.197 = bf16[2,128,1024]{2,1,0:T(8,128)(2,1)} all-gather(bf16[1,128,1024]{2,1,0:T(8,128)(2,1)S(1)} %copy.74), channel_id=1, replica_groups=mesh['yh'=2,'x'=4,'z'=4,'yl'=2,'c'=2] {'yl'}, dimensions={0}, use_global_device_ids=true | all-gather | bytes 786432 | tf_op jit(solution)/shard_map/all_gather | solution.py:76
  754.7 9.4 all-reduce.5
  787.1 10.4 all-gather.87.cloned.1.call-done
  800.0 12.2 all-gather.89.cloned.1.call-done
  815.0 13.3 %all-gather.85.cloned.1.call-done = bf16[2,256,2048]{2,1,0:T(8,128)(2,1)} async-done(((bf16[2,128,2048]{2,1,0:T(8,128)(2,1)}), bf16[2,256,2048]{2,1,0:T(8,128)(2,1)}) %all-gather.85.cloned.1.call-update) | async-done | bytes 2097168 | tf_op jit(solution)/shard_map/all_gather | solution.py:77
  832.0 103.5 %concatenate.38 = bf16[3932736]{0:T(1024)(128)(2,1)} concatenate(bf16[524288]{0:T(1024)(128)(2,1)} %bitcast.272, bf16[262144]{0:T(1024)(128)(2,1)} %bitcast.291, bf16[262144]{0:T(1024)(128)(2,1)} %bitcast.292, bf16[524288]{0:T(1024)(128)(2,1)S(1)} %bitcast.271, bf16[786432]{0:T(1024)(128)(2,1)} %bitcast.261, bf16[786432]{0:T(1024)(128)(2,1)} %bitcast.262, ...), dimensions={0} | concatenate | bytes 15730944 | tf_op jit(solution)/shard_map/concatenate | solution.py:82
  943.9 78.1 %reduce-scatter.3.cloned.1.call-done = bf16[7744,128]{1,0:T(8,128)(2,1)} async-done(((bf16[30976,128]{1,0:T(8,128)(2,1)}), bf16[7744,128]{1,0:T(8,128)(2,1)}) %reduce-scatter.3.cloned.1.call-update) | async-done | bytes 1982480 | tf_op jit(solution)/shard_map/reduce_scatter | solution.py:87
  1022.0 30.6 %reduce-scatter.5.cloned.1.call-done = bf16[1936,128]{1,0:T(8,128)(2,1)} async-done(((bf16[7744,128]{1,0:T(8,128)(2,1)}), bf16[1936,128]{1,0:T(8,128)(2,1)}) %reduce-scatter.5.cloned.1.call-update) | async-done | bytes 495632 | tf_op jit(solution)/shard_map/reduce_scatter | solution.py:88
  1052.7 37.9 %all-reduce.8.cloned.1.call-done = bf16[1936,128]{1,0:T(8,128)(2,1)} async-done(((bf16[1936,128]{1,0:T(8,128)(2,1)}), bf16[1936,128]{1,0:T(8,128)(2,1)}) %all-reduce.8.cloned.1.call-update) | async-done | bytes 495632 | tf_op jit(solution)/shard_map/psum | solution.py:89
  1091.0 31.0 %all-gather.53.cloned.1.call-done = bf16[7744,128]{1,0:T(8,128)(2,1)} async-done(((bf16[1936,128]{1,0:T(8,128)(2,1)}), bf16[7744,128]{1,0:T(8,128)(2,1)}) %all-gather.53.cloned.1.call-update) | async-done | bytes 1982480 | tf_op jit(solution)/shard_map/all_gather | solution.py:90
  1127.7 75.5 %all-gather.55.cloned.1.call-done = bf16[30976,128]{1,0:T(8,128)(2,1)} async-done(((bf16[7744,128]{1,0:T(8,128)(2,1)}), bf16[30976,128]{1,0:T(8,128)(2,1)}) %all-gather.55.cloned.1.call-update) | async-done | bytes 7929872 | tf_op jit(solution)/shard_map/all_gather | solution.py:91
  (287 shorter events, 259.2 us)
Async XLA Ops:
  7.9 55.3 %all-gather.65.cloned.1.call-start = ((), (), s32[]{:S(2)}) async-start(), calls=%async_computation.20 | async-start | bytes 1572864 | tf_op jit(solution)/shard_map/all_gather | solution.py:76
  8.7 92.9 %all-gather.57.cloned.1.call-start = ((), (), s32[]{:S(2)}) async-start(), calls=%async_computation.16 | async-start | bytes 3145728 | tf_op jit(solution)/shard_map/all_gather | solution.py:76
  9.4 130.3 %all-gather.69.cloned.1.call-start = ((), (), s32[]{:S(2)}) async-start(), calls=%async_computation.22 | async-start | bytes 3145728 | tf_op jit(solution)/shard_map/all_gather | solution.py:76
  10.0 179.7 %all-gather.73.cloned.1.call-start = ((), (), s32[]{:S(2)}) async-start(), calls=%async_computation.24 | async-start | bytes 4718592 | tf_op jit(solution)/shard_map/all_gather | solution.py:76
  10.6 229.1 %all-gather.77.cloned.1.call-start = ((), (), s32[]{:S(2)}) async-start(), calls=%async_computation.26 | async-start | bytes 4718592 | tf_op jit(solution)/shard_map/all_gather | solution.py:76
  11.1 244.9 %all-gather.63.cloned.1.call-start = ((), (), s32[]{:S(2)}) async-start(), calls=%async_computation.19 | async-start | bytes 3145728 | tf_op jit(solution)/shard_map/all_gather | solution.py:77
  36.8 235.6 %all-gather.67.cloned.1.call-start = ((), (), s32[]{:S(2)}) async-start(), calls=%async_computation.21 | async-start | bytes 3145728 | tf_op jit(solution)/shard_map/all_gather | solution.py:77
  63.3 228.5 %all-gather.59.cloned.1.call-start = ((), (), s32[]{:S(2)}) async-start(), calls=%async_computation.17 | async-start | bytes 6291456 | tf_op jit(solution)/shard_map/all_gather | solution.py:77
  101.6 274.4 %all-gather.81.cloned.1.call-start = ((), (), s32[]{:S(2)}) async-start(), calls=%async_computation.28 | async-start | bytes 4718592 | tf_op jit(solution)/shard_map/all_gather | solution.py:76
  102.2 354.4 %all-gather.71.cloned.1.call-start = ((), (), s32[]{:S(2)}) async-start(), calls=%async_computation.23 | async-start | bytes 6291456 | tf_op jit(solution)/shard_map/all_gather | solution.py:77
  139.7 320.7 %all-gather.75.cloned.1.call-start = ((), (), s32[]{:S(2)}) async-start(), calls=%async_computation.25 | async-start | bytes 9437184 | tf_op jit(solution)/shard_map/all_gather | solution.py:77
  189.7 276.7 %all-gather.79.cloned.1.call-start = ((), (), s32[]{:S(2)}) async-start(), calls=%async_computation.27 | async-start | bytes 9437184 | tf_op jit(solution)/shard_map/all_gather | solution.py:77
  309.3 66.7 %all-to-all-start = ((bf16[32,128,384]{2,1,0:T(8,128)(2,1)}), bf16[32,128,384]{2,1,0:T(8,128)(2,1)}, u32[]{:S(2)}, u32[]{:S(2)}) async-start(bf16[32,128,384]{2,1,0:T(8,128)(2,1)} %pad_maximum_fusion), calls=%async_computation | async-start | bytes 6291456 | tf_op jit(solution)/shard_map/all_to_all | solution.py:157
  318.9 152.4 %all-gather.83.cloned.1.call-start = ((), (), s32[]{:S(2)}) async-start(), calls=%async_computation.29 | async-start | bytes 9437184 | tf_op jit(solution)/shard_map/all_gather | solution.py:77
  497.6 48.9 %all-to-all-start.2 = ((bf16[32,128,128]{1,2,0:T(8,128)(2,1)}), bf16[32,128,128]{1,2,0:T(8,128)(2,1)}, u32[]{:S(2)}, u32[]{:S(2)}) async-start(bf16[32,128,128]{1,2,0:T(8,128)(2,1)} %bitcast_select_fusion.2), calls=%async_computation.2 | async-start | bytes 2097152 | tf_op jit(solution)/shard_map/all_to_all | solution.py:157
  503.1 175.5 %all-gather.93.cloned.1.call-start = ((), (), s32[]{:S(2)}) async-start(), calls=%async_computation.34 | async-start | bytes 2359296 | tf_op jit(solution)/shard_map/all_gather | solution.py:76
  608.4 54.4 %all-to-all-start.3 = ((bf16[32,128,384]{1,2,0:T(8,128)(2,1)}), bf16[32,128,384]{1,2,0:T(8,128)(2,1)}, u32[]{:S(2)}, u32[]{:S(2)}) async-start(bf16[32,128,384]{1,2,0:T(8,128)(2,1)} %pad_maximum_fusion.1), calls=%async_computation.3 | async-start | bytes 6291456 | tf_op jit(solution)/shard_map/all_to_all | solution.py:157
  617.7 61.4 %all-gather.97.cloned.1.call-start = ((), (), s32[]{:S(2)}) async-start(), calls=%async_computation.36 | async-start | bytes 2359296 | tf_op jit(solution)/shard_map/all_gather | solution.py:76
  618.3 117.1 %all-gather.101.cloned.1.call-start = ((), (), s32[]{:S(2)}) async-start(), calls=%async_computation.38 | async-start | bytes 1572864 | tf_op jit(solution)/shard_map/all_gather | solution.py:77
  662.8 76.7 %all-gather.51.cloned.1.call-start = ((), (), s32[]{:S(2)}) async-start(), calls=%async_computation.10 | async-start | bytes 1572864 | tf_op jit(solution)/shard_map/all_gather | solution.py:76
  668.0 79.1 %all-gather.91.cloned.1.call-start = ((), (), s32[]{:S(2)}) async-start(), calls=%async_computation.33 | async-start | bytes 1572864 | tf_op jit(solution)/shard_map/all_gather | solution.py:77
  678.5 91.6 %all-gather.95.cloned.1.call-start = ((), (), s32[]{:S(2)}) async-start(), calls=%async_computation.35 | async-start | bytes 4718592 | tf_op jit(solution)/shard_map/all_gather | solution.py:77
  679.1 103.6 %all-gather.99.cloned.1.call-start = ((), (), s32[]{:S(2)}) async-start(), calls=%async_computation.37 | async-start | bytes 4718592 | tf_op jit(solution)/shard_map/all_gather | solution.py:77
  679.8 117.6 %all-gather.87.cloned.1.call-start = ((), (), s32[]{:S(2)}) async-start(), calls=%async_computation.31 | async-start | bytes 1572864 | tf_op jit(solution)/shard_map/all_gather | solution.py:77
  691.7 34.1 %all-to-all-start.7 = ((bf16[128,4,768]{2,0,1:T(8,128)(2,1)}), bf16[128,4,768]{2,0,1:T(8,128)(2,1)}, u32[]{:S(2)}, u32[]{:S(2)}) async-start(bf16[128,4,768]{2,0,1:T(8,128)(2,1)} %bitcast.239), calls=%async_computation.7 | async-start | bytes 1572864 | tf_op jit(solution)/shard_map/all_to_all | solution.py:295
  701.0 111.2 %all-gather.89.cloned.1.call-start = ((), (), s32[]{:S(2)}) async-start(), calls=%async_computation.32 | async-start | bytes 1572864 | tf_op jit(solution)/shard_map/all_gather | solution.py:77
  731.9 96.5 %all-gather.85.cloned.1.call-start = ((), (), s32[]{:S(2)}) async-start(), calls=%async_computation.30 | async-start | bytes 3145728 | tf_op jit(solution)/shard_map/all_gather | solution.py:77
  770.1 251.9 %reduce-scatter.3.cloned.1.call-start = ((), (), s32[]{:S(2)}) async-start(), calls=%async_computation.11 | async-start | bytes 9912320 | tf_op jit(solution)/shard_map/reduce_scatter | solution.py:87
  943.8 108.8 %reduce-scatter.5.cloned.1.call-start = ((), (), s32[]{:S(2)}) async-start(), calls=%async_computation.12 | async-start | bytes 2478080 | tf_op jit(solution)/shard_map/reduce_scatter | solution.py:88
  1022.0 68.6 %all-reduce.8.cloned.1.call-start = ((), (), s32[]{:S(2)}) async-start(), calls=%async_computation.13 | async-start | bytes 991232 | tf_op jit(solution)/shard_map/psum | solution.py:89
  1052.7 69.3 %all-gather.53.cloned.1.call-start = ((), (), s32[]{:S(2)}) async-start(), calls=%async_computation.14 | async-start | bytes 2478080 | tf_op jit(solution)/shard_map/all_gather | solution.py:90
  1090.7 112.6 %all-gather.55.cloned.1.call-start = ((), (), s32[]{:S(2)}) async-start(), calls=%async_computation.15 | async-start | bytes 9912320 | tf_op jit(solution)/shard_map/all_gather | solution.py:91
  (44 other events, 1040.6 us)
Sparse Core Ops, SparseCore 0:
  9.7 27.0 all-gather.60
  38.4 24.7 all-gather.64
  64.9 36.6 all-gather.56
  103.0 36.6 all-gather.68
  141.2 48.4 all-gather.72
  191.2 48.4 all-gather.76
  241.3 14.6 all-gather.62
  257.7 14.6 all-gather.66
  274.0 17.6 all-gather.58
  293.2 82.6 all-gather.80
  377.6 21.7 all-gather.70
  400.9 20.8 all-gather.74
  423.4 20.7 all-gather.78
  445.7 20.7 all-gather.82
  546.6 31.9 all-gather.92
  620.5 57.1 all-gather.96
  679.2 15.1 all-gather.100
  696.5 32.6 all-gather.50
  730.9 16.0 all-gather.90
  748.5 16.2 all-gather.94
  766.5 16.1 all-gather.98
  784.3 13.0 all-gather.86
  799.1 13.0 all-gather.88
  813.7 14.6 all-gather.84
  944.0 77.9 reduce-scatter.2
  1024.2 28.3 reduce-scatter.4
  1055.1 35.4 all-reduce.7
  1092.4 29.5 all-gather.52
  1123.7 79.5 all-gather.54
where the time goes:
time: 1260 us; the launch traced here: 1240 us
  waiting for transfers between devices  631 us (50%)
  local copies, waits for them, and re-layouts  204 us (16%)
  matrix products  146 us (12%)
  blocking collectives  122 us (10%)
  other arithmetic  69.1 us (5%)
  starting transfers between devices  51.6 us (4%)
  between operations  16.7 us (1%)
    all_gather x10, waiting for transfers between devices, gather_fsdp(): across = lax.all_gather(values, 'yl', axis=0, tiled=False)  284 us
    concatenate x1, local copies, waits for them, and re-layouts, reduce_ctx(): flat = jnp.concatenate([s.astype(jnp.bfloat16).reshape(-1) for s in shards])  104 us
    all_gather x14, waiting for transfers between devices, gather_fsdp(): both = lax.all_gather(across, 'c', axis=1, tiled=False)  87.8 us
    all_gather x4, blocking collectives, gather_fsdp(): across = lax.all_gather(values, 'yl', axis=0, tiled=False)  83.6 us
    reduce_scatter x1, waiting for transfers between devices, reduce_ctx(): part = lax.psum_scatter(flat, 'z', scatter_dimension=0, tiled=True)  78.1 us
    all_gather x1, waiting for transfers between devices, reduce_ctx(): full = lax.all_gather(part, 'z', axis=0, tiled=True).reshape(-1)  75.5 us
    dot_general x8, matrix products, right_dot(): lax.dot_general(left_side, right_side, (((1,), (1,)), ((), ())), preferre...  45.2 us
    psum x1, waiting for transfers between devices, reduce_ctx(): part = lax.psum(part, 'yh')  37.9 us
  transfers between devices with their start and end apart: 36, of which 21 were waited for; matrix products, arithmetic and copies ran while one was open for 20% of the time, Pallas kernels for 0%

commit v1 on v0

--- a/solution.py
+++ b/solution.py
@@ -12,6 +12,13 @@
 EPSILON = 1e-06
 THETA = 1000000.0
 MASKED = -1e30
+
+
+def gather_over(x, axis, d):
+    count = lax.axis_size(axis)
+    shards = jnp.stack([x for _ in range(count)])
+    shards = lax.all_to_all(shards, axis, split_axis=0, concat_axis=0)
+    return jnp.concatenate(shards, axis=d)
 
 
 def rms_apply(values, norm_gain):
@@ -88,7 +95,7 @@
     part = lax.psum_scatter(part, "x", scatter_dimension=0, tiled=True)
     part = lax.psum(part, "yh")
     part = lax.all_gather(part, "x", axis=0, tiled=True)
-    full = lax.all_gather(part, "z", axis=0, tiled=True).reshape(-1)
+    full = gather_over(part, "z", 0).reshape(-1)
     out = []
     at = 0
     for s in shards:

time: 1260 us -> 1300 us (1.032)
  local copies, waits for them, and re-layouts: 204 us -> 224 us
    all_to_all x0 -> x1, waiting for transfers between devices: none -> 82.5 us  [gather_over(): shards = lax.all_to_all(shards, axis, split_axis=0, concat_axis=0)]
    all_gather x1 -> x0, waiting for transfers between devices: 75.5 us -> none  [reduce_ctx(): full = lax.all_gather(part, 'z', axis=0, tiled=True).reshape(-1)]
    slice x0 -> x2, local copies, waits for them, and re-layouts: none -> 25.6 us  [reduce_ctx(): out.append(full[at:at + s.size].reshape(s.shape).astype(jnp.float32))]
  transfers between devices with their start and end apart: 36 -> 36, of which waited for: 21 -> 21; matrix products, arithmetic and copies ran while one was open for 20% -> 19% of each run, Pallas kernels for 0% -> 0%
where the time goes in v1:
time: 1300 us; the launch traced here: 1280 us
  waiting for transfers between devices  638 us (49%)
  local copies, waits for them, and re-layouts  224 us (17%)
  matrix products  146 us (11%)
  blocking collectives  122 us (9%)
  other arithmetic  74.7 us (6%)
  starting transfers between devices  57.1 us (4%)
  between operations  16.9 us (1%)
    all_gather x10, waiting for transfers between devices, gather_fsdp(): across = lax.all_gather(values, 'yl', axis=0, tiled=False)  284 us
    concatenate x1, local copies, waits for them, and re-layouts, reduce_ctx(): flat = jnp.concatenate([s.astype(jnp.bfloat16).reshape(-1) for s in shards])  104 us
    all_gather x14, waiting for transfers between devices, gather_fsdp(): both = lax.all_gather(across, 'c', axis=1, tiled=False)  87.8 us
    all_gather x4, blocking collectives, gather_fsdp(): across = lax.all_gather(values, 'yl', axis=0, tiled=False)  83.6 us
    all_to_all x1, waiting for transfers between devices, gather_over(): shards = lax.all_to_all(shards, axis, split_axis=0, concat_axis=0)  82.5 us
    reduce_scatter x1, waiting for transfers between devices, reduce_ctx(): part = lax.psum_scatter(flat, 'z', scatter_dimension=0, tiled=True)  78.1 us
    dot_general x8, matrix products, right_dot(): lax.dot_general(left_side, right_side, (((1,), (1,)), ((), ())), preferre...  45.2 us
    psum x1, waiting for transfers between devices, reduce_ctx(): part = lax.psum(part, 'yh')  37.7 us
  transfers between devices with their start and end apart: 36, of which 21 were waited for; matrix products, arithmetic and copies ran while one was open for 19% of the time, Pallas kernels for 0%

profile of v1, /device:TPU:1, one launch (start us, length us, event | category | flops | bytes accessed | tf_op | source)
XLA Modules:
  0.0 1279.2 jit_solution(8685085691142303264)
XLA Ops:
  11.2 25.6 %all-gather.58.cloned.1.call-done = bf16[512,1024]{1,0:T(8,128)(2,1)} async-done(((bf16[256,1024]{1,0:T(8,128)(2,1)}), bf16[512,1024]{1,0:T(8,128)(2,1)}) %all-gather.58.cloned.1.call-update) | async-done | bytes 1048592 | tf_op jit(solution)/shard_map/all_gather | solution.py:83
  36.8 26.4 %all-gather.62.cloned.1.call-done = bf16[512,1024]{1,0:T(8,128)(2,1)} async-done(((bf16[256,1024]{1,0:T(8,128)(2,1)}), bf16[512,1024]{1,0:T(8,128)(2,1)}) %all-gather.62.cloned.1.call-update) | async-done | bytes 1048592 | tf_op jit(solution)/shard_map/all_gather | solution.py:83
  63.3 38.2 %all-gather.54.cloned.1.call-done = bf16[512,2048]{1,0:T(8,128)(2,1)} async-done(((bf16[256,2048]{1,0:T(8,128)(2,1)}), bf16[512,2048]{1,0:T(8,128)(2,1)}) %all-gather.54.cloned.1.call-update) | async-done | bytes 2097168 | tf_op jit(solution)/shard_map/all_gather | solution.py:83
  102.2 37.5 %all-gather.66.cloned.1.call-done = bf16[1024,1024]{1,0:T(8,128)(2,1)} async-done(((bf16[512,1024]{1,0:T(8,128)(2,1)}), bf16[1024,1024]{1,0:T(8,128)(2,1)}) %all-gather.66.cloned.1.call-update) | async-done | bytes 2097168 | tf_op jit(solution)/shard_map/all_gather | solution.py:83
  139.8 49.9 %all-gather.70.cloned.1.call-done = bf16[512,3072]{1,0:T(8,128)(2,1)} async-done(((bf16[256,3072]{1,0:T(8,128)(2,1)}), bf16[512,3072]{1,0:T(8,128)(2,1)}) %all-gather.70.cloned.1.call-update) | async-done | bytes 3145744 | tf_op jit(solution)/shard_map/all_gather | solution.py:83
  190.3 49.3 %all-gather.74.cloned.1.call-done = bf16[512,3072]{1,0:T(8,128)(2,1)} async-done(((bf16[256,3072]{1,0:T(8,128)(2,1)}), bf16[512,3072]{1,0:T(8,128)(2,1)}) %all-gather.74.cloned.1.call-update) | async-done | bytes 3145744 | tf_op jit(solution)/shard_map/all_gather | solution.py:83
  239.9 16.1 %all-gather.60.cloned.1.call-done = bf16[2,512,1024]{2,1,0:T(8,128)(2,1)} async-done(((bf16[2,256,1024]{2,1,0:T(8,128)(2,1)}), bf16[2,512,1024]{2,1,0:T(8,128)(2,1)}) %all-gather.60.cloned.1.call-update) | async-done | bytes 2097168 | tf_op jit(solution)/shard_map/all_gather | solution.py:84
  261.1 11.2 all-gather.64.cloned.1.call-done
  278.2 13.5 %all-gather.56.cloned.1.call-done = bf16[2,512,2048]{2,1,0:T(8,128)(2,1)} async-done(((bf16[2,256,2048]{2,1,0:T(8,128)(2,1)}), bf16[2,512,2048]{2,1,0:T(8,128)(2,1)}) %all-gather.56.cloned.1.call-update) | async-done | bytes 4194320 | tf_op jit(solution)/shard_map/all_gather | solution.py:84
  319.2 56.7 %all-gather.78.cloned.1.call-done = bf16[1536,1024]{1,0:T(8,128)(2,1)} async-done(((bf16[768,1024]{1,0:T(8,128)(2,1)}), bf16[1536,1024]{1,0:T(8,128)(2,1)}) %all-gather.78.cloned.1.call-update) | async-done | bytes 3145744 | tf_op jit(solution)/shard_map/all_gather | solution.py:83
  378.1 14.4 %fusion.47 = (f32[2048]{0:T(1024)S(1)}, f32[2048,4096]{1,0:T(8,128)}) fusion(s32[2048]{0:T(1024)S(1)} %dynamic_slice.18, s32[4096]{0:T(1024)S(1)} %add.146, bf16[2048,128]{1,0:T(8,128)(2,1)S(1)} %bitcast.302, bf16[4096,128]{1,0:T(8,128)(2,1)S(1)} %bitcast.296), kind=kOutput, calls=%fused_computation.146 | convolution fusion | flops 2181036032 | bytes 35160064 | tf_op jit(solution)/shard_map/qd,kd->qk/dot_general | solution.py:206
  392.5 16.1 %exponential_reduce_fusion = f32[2048]{0:T(1024)S(1)} fusion(f32[2048]{0:T(1024)S(1)} %get-tuple-element.53, f32[2048,4096]{1,0:T(8,128)} %get-tuple-element.54, s32[2048]{0:T(1024)S(1)} %dynamic_slice.18, s32[4096]{0:T(1024)S(1)} %add.146), kind=kLoop, calls=%fused_computation.6 | loop fusion | flops 41940992 | bytes 33595392 | tf_op jit(solution)/shard_map/reduce_sum | solution.py:213
  408.6 18.5 %fusion.49 = (bf16[2048,128]{1,0:T(8,128)(2,1)S(1)}, f32[2048,128]{1,0:T(8,128)}) fusion(bf16[4096,128]{1,0:T(8,128)(2,1)S(1)} %bitcast.298, f32[2048]{0:T(1024)S(1)} %log_add_fusion, f32[2048,4096]{1,0:T(8,128)} %get-tuple-element.54, s32[2048]{0:T(1024)S(1)} %dynamic_slice.18, s32[4096]{0:T(1024)S(1)} %add.146), kind=kOutput, calls=%fused_computation.148 | convolution fusion | flops 2189688832 | bytes 36208640 | tf_op jit(solution)/shard_map/dot_general | solution.py:215
  427.5 29.0 %all_to_all.98 = bf16[32,128,128]{1,2,0:T(8,128)(2,1)S(1)} all-to-all(bf16[32,128,128]{1,2,0:T(8,128)(2,1)S(1)} %bitcast_select_fusion.3), channel_id=1, replica_groups=mesh['yh'=2,'x'=4,'z'=4,'yl'=2,'c'=2] {'yh','x','z'}, dimensions={0} | all-to-all | bytes 2097152 | tf_op jit(solution)/shard_map/all_to_all | solution.py:164
  503.5 20.3 %fusion.2 = bf16[4096,2048]{0,1:T(8,128)(2,1)} fusion(f32[2048,4096]{1,0:T(8,128)} %get-tuple-element.54, f32[2048]{0:T(1024)S(1)} %log_add_fusion, s32[4096]{0:T(1024)S(1)} %add.146, s32[2048]{0:T(1024)S(1)} %dynamic_slice.18), kind=kLoop, calls=%fused_computation.3 | loop fusion | flops 41943040 | bytes 50364416 | tf_op jit(solution)/shard_map/convert_element_type | solution.py:214
  523.9 22.6 %copy.81 = bf16[4096,2048]{1,0:T(8,128)(2,1)} copy(bf16[4096,2048]{0,1:T(8,128)(2,1)} %fusion.2) | data formatting | bytes 33554432 | tf_op jit(solution)/shard_map/dot_general | solution.py:71
  551.3 20.5 %multiply_convert_fusion = bf16[2048,4096]{1,0:T(8,128)(2,1)} fusion(f32[2048]{0:T(1024)S(1)} %multiply_reduce_fusion.2, f32[2048]{0:T(1024)S(1)} %log_add_fusion, bf16[2048,128]{1,0:T(8,128)(2,1)S(1)} %bitcast.254, bf16[4096,128]{1,0:T(8,128)(2,1)} %bitcast.299, f32[2048,4096]{1,0:T(8,128)} %get-tuple-element.54, s32[2048]{0:T(1024)S(1)} %dynamic_slice.18, ...), kind=kOutput, calls=%fused_computation.4 | convolution fusion | flops 2206203904 | bytes 51945472 | tf_op jit(solution)/shard_map/dot_general | solution.py:77
  595.0 10.3 convolution_convert_fusion.6
  618.4 44.4 %all_gather.209 = bf16[2,128,1024]{2,1,0:T(8,128)(2,1)} all-gather(bf16[1,128,1024]{2,1,0:T(8,128)(2,1)S(1)} %copy-done.15), channel_id=1, replica_groups=mesh['yh'=2,'x'=4,'z'=4,'yl'=2,'c'=2] {'yl'}, dimensions={0}, use_global_device_ids=true | all-gather | bytes 786432 | tf_op jit(solution)/shard_map/all_gather | solution.py:83
  668.0 10.4 all-gather.17
  702.2 22.3 %all_gather.194 = bf16[2,128,1024]{2,1,0:T(8,128)(2,1)} all-gather(bf16[1,128,1024]{2,1,0:T(8,128)(2,1)S(1)} %copy.74), channel_id=1, replica_groups=mesh['yh'=2,'x'=4,'z'=4,'yl'=2,'c'=2] {'yl'}, dimensions={0}, use_global_device_ids=true | all-gather | bytes 786432 | tf_op jit(solution)/shard_map/all_gather | solution.py:83
  787.1 10.4 all-gather.84.cloned.1.call-done
  800.0 12.2 all-gather.86.cloned.1.call-done
  815.1 13.3 %all-gather.82.cloned.1.call-done = bf16[2,256,2048]{2,1,0:T(8,128)(2,1)} async-done(((bf16[2,128,2048]{2,1,0:T(8,128)(2,1)}), bf16[2,256,2048]{2,1,0:T(8,128)(2,1)}) %all-gather.82.cloned.1.call-update) | async-done | bytes 2097168 | tf_op jit(solution)/shard_map/all_gather | solution.py:84
  832.0 103.6 %concatenate.38 = bf16[3932736]{0:T(1024)(128)(2,1)} concatenate(bf16[524288]{0:T(1024)(128)(2,1)} %bitcast.261, bf16[262144]{0:T(1024)(128)(2,1)} %bitcast.280, bf16[262144]{0:T(1024)(128)(2,1)} %bitcast.281, bf16[524288]{0:T(1024)(128)(2,1)S(1)} %bitcast.260, bf16[786432]{0:T(1024)(128)(2,1)} %bitcast.250, bf16[786432]{0:T(1024)(128)(2,1)} %bitcast.251, ...), dimensions={0} | concatenate | bytes 15730944 | tf_op jit(solution)/shard_map/concatenate | solution.py:89
  943.9 78.1 %reduce-scatter.3.cloned.1.call-done = bf16[7744,128]{1,0:T(8,128)(2,1)} async-done(((bf16[30976,128]{1,0:T(8,128)(2,1)}), bf16[7744,128]{1,0:T(8,128)(2,1)}) %reduce-scatter.3.cloned.1.call-update) | async-done | bytes 1982480 | tf_op jit(solution)/shard_map/reduce_scatter | solution.py:94
  1022.1 30.6 %reduce-scatter.5.cloned.1.call-done = bf16[1936,128]{1,0:T(8,128)(2,1)} async-done(((bf16[7744,128]{1,0:T(8,128)(2,1)}), bf16[1936,128]{1,0:T(8,128)(2,1)}) %reduce-scatter.5.cloned.1.call-update) | async-done | bytes 495632 | tf_op jit(solution)/shard_map/reduce_scatter | solution.py:95
  1053.0 37.7 %all-reduce.8.cloned.1.call-done = bf16[1936,128]{1,0:T(8,128)(2,1)} async-done(((bf16[1936,128]{1,0:T(8,128)(2,1)}), bf16[1936,128]{1,0:T(8,128)(2,1)}) %all-reduce.8.cloned.1.call-update) | async-done | bytes 495632 | tf_op jit(solution)/shard_map/psum | solution.py:96
  1090.7 31.3 %all-gather.52.cloned.1.call-done = bf16[7744,128]{1,0:T(8,128)(2,1)} async-done(((bf16[1936,128]{1,0:T(8,128)(2,1)}), bf16[7744,128]{1,0:T(8,128)(2,1)}) %all-gather.52.cloned.1.call-update) | async-done | bytes 1982480 | tf_op jit(solution)/shard_map/all_gather | solution.py:97
  1139.1 82.5 %all-to-all-done.8 = bf16[4,7744,128]{2,1,0:T(8,128)(2,1)} async-done(((bf16[4,7744,128]{2,1,0:T(8,128)(2,1)}), bf16[4,7744,128]{2,1,0:T(8,128)(2,1)}, u32[]{:S(2)}, u32[]{:S(2)}) %all-to-all-start.8) | async-done | bytes 7929888 | tf_op jit(solution)/shard_map/all_to_all | solution.py:20
  1221.6 12.8 %slice.103 = bf16[3872,1024]{1,0:T(8,128)(2,1)} reshape(bf16[4,7744,128]{2,1,0:T(8,128)(2,1)} %all-to-all-done.8) | data formatting | bytes 15859712 | tf_op jit(solution)/shard_map/slice | solution.py:102
  1250.1 12.8 %slice.101 = bf16[1936,2048]{1,0:T(8,128)(2,1)} reshape(bf16[4,7744,128]{2,1,0:T(8,128)(2,1)} %all-to-all-done.8) | data formatting | bytes 15859712 | tf_op jit(solution)/shard_map/slice | solution.py:102
  (286 shorter events, 283.8 us)
Async XLA Ops:
  7.9 55.3 %all-gather.62.cloned.1.call-start = ((), (), s32[]{:S(2)}) async-start(), calls=%async_computation.20 | async-start | bytes 1572864 | tf_op jit(solution)/shard_map/all_gather | solution.py:83
  8.7 92.9 %all-gather.54.cloned.1.call-start = ((), (), s32[]{:S(2)}) async-start(), calls=%async_computation.16 | async-start | bytes 3145728 | tf_op jit(solution)/shard_map/all_gather | solution.py:83
  9.4 130.3 %all-gather.66.cloned.1.call-start = ((), (), s32[]{:S(2)}) async-start(), calls=%async_computation.22 | async-start | bytes 3145728 | tf_op jit(solution)/shard_map/all_gather | solution.py:83
  10.0 179.7 %all-gather.70.cloned.1.call-start = ((), (), s32[]{:S(2)}) async-start(), calls=%async_computation.24 | async-start | bytes 4718592 | tf_op jit(solution)/shard_map/all_gather | solution.py:83
  10.6 229.1 %all-gather.74.cloned.1.call-start = ((), (), s32[]{:S(2)}) async-start(), calls=%async_computation.26 | async-start | bytes 4718592 | tf_op jit(solution)/shard_map/all_gather | solution.py:83
  11.1 244.9 %all-gather.60.cloned.1.call-start = ((), (), s32[]{:S(2)}) async-start(), calls=%async_computation.19 | async-start | bytes 3145728 | tf_op jit(solution)/shard_map/all_gather | solution.py:84
  36.8 235.6 %all-gather.64.cloned.1.call-start = ((), (), s32[]{:S(2)}) async-start(), calls=%async_computation.21 | async-start | bytes 3145728 | tf_op jit(solution)/shard_map/all_gather | solution.py:84
  63.3 228.5 %all-gather.56.cloned.1.call-start = ((), (), s32[]{:S(2)}) async-start(), calls=%async_computation.17 | async-start | bytes 6291456 | tf_op jit(solution)/shard_map/all_gather | solution.py:84
  101.6 274.3 %all-gather.78.cloned.1.call-start = ((), (), s32[]{:S(2)}) async-start(), calls=%async_computation.28 | async-start | bytes 4718592 | tf_op jit(solution)/shard_map/all_gather | solution.py:83
  102.2 354.4 %all-gather.68.cloned.1.call-start = ((), (), s32[]{:S(2)}) async-start(), calls=%async_computation.23 | async-start | bytes 6291456 | tf_op jit(solution)/shard_map/all_gather | solution.py:84
  139.7 320.7 %all-gather.72.cloned.1.call-start = ((), (), s32[]{:S(2)}) async-start(), calls=%async_computation.25 | async-start | bytes 9437184 | tf_op jit(solution)/shard_map/all_gather | solution.py:84
  189.7 276.7 %all-gather.76.cloned.1.call-start = ((), (), s32[]{:S(2)}) async-start(), calls=%async_computation.27 | async-start | bytes 9437184 | tf_op jit(solution)/shard_map/all_gather | solution.py:84
  309.3 66.6 %all-to-all-start = ((bf16[32,128,384]{2,1,0:T(8,128)(2,1)}), bf16[32,128,384]{2,1,0:T(8,128)(2,1)}, u32[]{:S(2)}, u32[]{:S(2)}) async-start(bf16[32,128,384]{2,1,0:T(8,128)(2,1)} %pad_maximum_fusion), calls=%async_computation | async-start | bytes 6291456 | tf_op jit(solution)/shard_map/all_to_all | solution.py:164
  318.9 152.4 %all-gather.80.cloned.1.call-start = ((), (), s32[]{:S(2)}) async-start(), calls=%async_computation.29 | async-start | bytes 9437184 | tf_op jit(solution)/shard_map/all_gather | solution.py:84
  497.6 48.9 %all-to-all-start.2 = ((bf16[32,128,128]{1,2,0:T(8,128)(2,1)}), bf16[32,128,128]{1,2,0:T(8,128)(2,1)}, u32[]{:S(2)}, u32[]{:S(2)}) async-start(bf16[32,128,128]{1,2,0:T(8,128)(2,1)} %bitcast_select_fusion.2), calls=%async_computation.2 | async-start | bytes 2097152 | tf_op jit(solution)/shard_map/all_to_all | solution.py:164
  503.1 175.5 %all-gather.90.cloned.1.call-start = ((), (), s32[]{:S(2)}) async-start(), calls=%async_computation.34 | async-start | bytes 2359296 | tf_op jit(solution)/shard_map/all_gather | solution.py:83
  608.4 54.4 %all-to-all-start.3 = ((bf16[32,128,384]{1,2,0:T(8,128)(2,1)}), bf16[32,128,384]{1,2,0:T(8,128)(2,1)}, u32[]{:S(2)}, u32[]{:S(2)}) async-start(bf16[32,128,384]{1,2,0:T(8,128)(2,1)} %pad_maximum_fusion.1), calls=%async_computation.3 | async-start | bytes 6291456 | tf_op jit(solution)/shard_map/all_to_all | solution.py:164
  617.7 61.4 %all-gather.94.cloned.1.call-start = ((), (), s32[]{:S(2)}) async-start(), calls=%async_computation.36 | async-start | bytes 2359296 | tf_op jit(solution)/shard_map/all_gather | solution.py:83
  618.3 117.1 %all-gather.98.cloned.1.call-start = ((), (), s32[]{:S(2)}) async-start(), calls=%async_computation.38 | async-start | bytes 1572864 | tf_op jit(solution)/shard_map/all_gather | solution.py:84
  662.8 76.7 %all-gather.50.cloned.1.call-start = ((), (), s32[]{:S(2)}) async-start(), calls=%async_computation.11 | async-start | bytes 1572864 | tf_op jit(solution)/shard_map/all_gather | solution.py:83
  668.0 79.1 %all-gather.88.cloned.1.call-start = ((), (), s32[]{:S(2)}) async-start(), calls=%async_computation.33 | async-start | bytes 1572864 | tf_op jit(solution)/shard_map/all_gather | solution.py:84
  678.5 91.6 %all-gather.92.cloned.1.call-start = ((), (), s32[]{:S(2)}) async-start(), calls=%async_computation.35 | async-start | bytes 4718592 | tf_op jit(solution)/shard_map/all_gather | solution.py:84
  679.0 103.6 %all-gather.96.cloned.1.call-start = ((), (), s32[]{:S(2)}) async-start(), calls=%async_computation.37 | async-start | bytes 4718592 | tf_op jit(solution)/shard_map/all_gather | solution.py:84
  679.8 117.6 %all-gather.84.cloned.1.call-start = ((), (), s32[]{:S(2)}) async-start(), calls=%async_computation.31 | async-start | bytes 1572864 | tf_op jit(solution)/shard_map/all_gather | solution.py:84
  691.7 34.1 %all-to-all-start.7 = ((bf16[128,4,768]{2,0,1:T(8,128)(2,1)}), bf16[128,4,768]{2,0,1:T(8,128)(2,1)}, u32[]{:S(2)}, u32[]{:S(2)}) async-start(bf16[128,4,768]{2,0,1:T(8,128)(2,1)} %bitcast.229), calls=%async_computation.7 | async-start | bytes 1572864 | tf_op jit(solution)/shard_map/all_to_all | solution.py:302
  701.0 111.2 %all-gather.86.cloned.1.call-start = ((), (), s32[]{:S(2)}) async-start(), calls=%async_computation.32 | async-start | bytes 1572864 | tf_op jit(solution)/shard_map/all_gather | solution.py:84
  731.9 96.5 %all-gather.82.cloned.1.call-start = ((), (), s32[]{:S(2)}) async-start(), calls=%async_computation.30 | async-start | bytes 3145728 | tf_op jit(solution)/shard_map/all_gather | solution.py:84
  770.1 251.9 %reduce-scatter.3.cloned.1.call-start = ((), (), s32[]{:S(2)}) async-start(), calls=%async_computation.12 | async-start | bytes 9912320 | tf_op jit(solution)/shard_map/reduce_scatter | solution.py:94
  943.9 108.8 %reduce-scatter.5.cloned.1.call-start = ((), (), s32[]{:S(2)}) async-start(), calls=%async_computation.13 | async-start | bytes 2478080 | tf_op jit(solution)/shard_map/reduce_scatter | solution.py:95
  1022.0 68.6 %all-reduce.8.cloned.1.call-start = ((), (), s32[]{:S(2)}) async-start(), calls=%async_computation.14 | async-start | bytes 991232 | tf_op jit(solution)/shard_map/psum | solution.py:96
  1052.7 69.3 %all-gather.52.cloned.1.call-start = ((), (), s32[]{:S(2)}) async-start(), calls=%async_computation.15 | async-start | bytes 2478080 | tf_op jit(solution)/shard_map/all_gather | solution.py:97
  1127.7 93.9 %all-to-all-start.8 = ((bf16[4,7744,128]{2,1,0:T(8,128)(2,1)}), bf16[4,7744,128]{2,1,0:T(8,128)(2,1)}, u32[]{:S(2)}, u32[]{:S(2)}) async-start(bf16[4,7744,128]{2,1,0:T(8,128)(2,1)} %stack.2), calls=%async_computation.10 | async-start | bytes 15859712 | tf_op jit(solution)/shard_map/all_to_all | solution.py:20
  (44 other events, 868.1 us)
Sparse Core Ops, SparseCore 0:
  9.7 27.0 all-gather.57
  38.4 24.7 all-gather.61
  64.9 36.6 all-gather.53
  103.0 36.6 all-gather.65
  141.2 48.4 all-gather.69
  191.2 48.4 all-gather.73
  241.3 14.6 all-gather.59
  257.7 14.6 all-gather.63
  274.0 17.6 all-gather.55
  293.2 82.5 all-gather.77
  377.5 21.7 all-gather.67
  400.9 20.8 all-gather.71
  423.4 20.7 all-gather.75
  445.7 20.7 all-gather.79
  546.6 31.9 all-gather.89
  620.5 57.1 all-gather.93
  679.2 15.2 all-gather.97
  696.5 32.6 all-gather.49
  730.9 16.0 all-gather.87
  748.5 16.2 all-gather.91
  766.5 16.1 all-gather.95
  784.3 13.0 all-gather.83
  799.1 13.0 all-gather.85
  813.7 14.6 all-gather.81
  944.0 77.9 reduce-scatter.2
  1024.3 28.3 reduce-scatter.4
  1055.1 35.4 all-reduce.7
  1092.4 29.5 all-gather.51
